TPU v7x, 128 devices: a whole 4x4x4 slice. The times are simulated.
128 devices in a mesh: section: 8 (over x, core), expert: 16 (over z, y).
Axes of the slice: x: 4, y: 4, z: 4, core: 2. Of those that a mesh axis runs over, the one named last changes fastest.
Arguments:
- sent_acts: bfloat16 [8, 2048, 6144], P('section', 'expert'), may hold values from -6 to 6
- sent_cots: bfloat16 [8, 2048, 6144], P('section', 'expert'), may hold values from -6 to 6
- expert_ids: int32 [8, 2048, 2], P('section', 'expert'), may hold values from 0 to 7, as said below
- gate_probs: float32 [8, 2048, 2], P('section', 'expert'), may hold values from 0.1 to 0.9
- gate_weight: bfloat16 [8, 6144, 8192], P('section', None, 'expert'), may hold values from -0.078125 to 0.078125
- up_weight: bfloat16 [8, 6144, 8192], P('section', None, 'expert'), may hold values from -0.078125 to 0.078125
- down_weight: bfloat16 [8, 8192, 6144], P('section', 'expert'), may hold values from -0.0625 to 0.0625
Outputs:
- out_acts: bfloat16 [8, 2048, 6144], P('section', 'expert')
- in_grads: bfloat16 [8, 2048, 6144], P('section', 'expert')
Inputs may be any that keep to these rules, and one draw needn't show every extreme that they name: `expert_ids`: in every section, at most 40 of the 128 tokens of one device name expert 0, and at least one device's tokens name it 40 times; a token's two experts differ.
All inputs are finite; a program needn't handle non-finite values.
Results may differ from a plain program's by a relative error of at most 0.015.
Values may be sent and summed in bfloat16 or wider, within the bound.
A program may use at most 128 MiB of HBM per device.

v0:
```python
import jax
import jax.numpy as jnp
from jax import lax
from jax.sharding import PartitionSpec as P

CAP = 40


def shifted(value, axis, steps):
    count = lax.axis_size(axis)
    pairs = [(source, (source + steps) % count) for source in range(count)]
    return lax.ppermute(value, axis, pairs)


def silu_grad(pre):
    sigma = jax.nn.sigmoid(pre)
    return sigma * (1.0 + pre * (1.0 - sigma))


def run_rows(kernel, inputs):
    return kernel(*inputs)


def combine(term_rows):
    return lax.psum_scatter(
        term_rows(jnp.int32(0), lax.axis_size("expert") * CAP).astype(jnp.bfloat16),
        "expert",
        scatter_dimension=0,
        tiled=True,
    ).astype(jnp.float32)


def body(sent_acts, sent_cots, expert_ids, gate_probs, gate_weight, up_weight, down_weight):
    tok_count = sent_acts.shape[1]
    gate_cols = gate_weight[0]
    up_cols = up_weight[0]
    down_rows = down_weight[0]
    contract = (((1,), (1,)), ((), ()))
    incoming = shifted(sent_acts[0], "section", 1)
    cot_in = shifted(sent_cots[0], "section", -1)
    chosen = expert_ids[0] == 0
    picked = jnp.any(chosen, axis=1)
    picked_int = picked.astype(jnp.int32)
    share = jnp.sum(jnp.where(chosen, gate_probs[0], 0.0), axis=1)
    ranking = jnp.cumsum(picked_int) - picked_int
    slot_of = jnp.where(picked, ranking, CAP)
    table = (
        jnp.full((CAP + 1,), -1, jnp.int32)
        .at[slot_of]
        .set(jnp.arange(tok_count, dtype=jnp.int32))[:CAP]
    )
    filled_slot = table >= 0
    source = jnp.maximum(table, 0)
    slot_acts = jnp.where(filled_slot[:, None], incoming[source], jnp.zeros((), incoming.dtype))
    all_acts = lax.all_gather(slot_acts, "expert", axis=0, tiled=True)

    def forward_rows(rows_in):
        pre_gate = jnp.dot(rows_in, gate_cols, preferred_element_type=jnp.float32)
        pre_up = jnp.dot(rows_in, up_cols, preferred_element_type=jnp.float32)
        hidden = (jax.nn.silu(pre_gate) * pre_up).astype(jnp.bfloat16)
        return (pre_gate, pre_up, hidden)

    pre_gate, pre_up, hidden = run_rows(forward_rows, (all_acts,))

    def forward_term(start, count):
        return jnp.dot(hidden, down_rows, preferred_element_type=jnp.float32)

    slot_out = combine(forward_term)
    back_index = jnp.minimum(slot_of, CAP - 1)
    out_acts = jnp.where(picked[:, None], share[:, None] * slot_out[back_index], 0.0).astype(
        jnp.bfloat16
    )
    out_grad = (cot_in.astype(jnp.float32) * share[:, None]).astype(jnp.bfloat16)
    slot_grads = jnp.where(filled_slot[:, None], out_grad[source], jnp.zeros((), out_grad.dtype))
    all_grads = lax.all_gather(slot_grads, "expert", axis=0, tiled=True)

    def backward_rows(gate_in, up_in, grads_in):
        hid_grad = lax.dot_general(
            grads_in, down_rows, contract, preferred_element_type=jnp.float32
        )
        gate_grad = (hid_grad * up_in * silu_grad(gate_in)).astype(jnp.bfloat16)
        up_grad = (hid_grad * jax.nn.silu(gate_in)).astype(jnp.bfloat16)
        return (gate_grad, up_grad)

    gate_grad, up_grad = run_rows(backward_rows, (pre_gate, pre_up, all_grads))

    def backward_term(start, count):
        term = lax.dot_general(gate_grad, gate_cols, contract, preferred_element_type=jnp.float32)
        return term + lax.dot_general(
            up_grad, up_cols, contract, preferred_element_type=jnp.float32
        )

    slot_back = combine(backward_term)
    in_grads = jnp.where(picked[:, None], slot_back[back_index], 0.0).astype(jnp.bfloat16)
    return (out_acts[None], in_grads[None])


def solution(mesh):
    placed = (
        P("section", "expert", None),
        P("section", "expert", None),
        P("section", "expert", None),
        P("section", "expert", None),
        P("section", None, "expert"),
        P("section", None, "expert"),
        P("section", "expert", None),
    )
    return jax.shard_map(
        body,
        mesh=mesh,
        in_specs=placed,
        out_specs=(P("section", "expert", None), P("section", "expert", None)),
        check_vma=False,
    )
```

profile of v0, /device:TPU:0, one launch (start us, length us, event | category | flops | bytes accessed | tf_op | source)
XLA Modules:
  0.0 396.9 jit_solution(13419910968165939987)
XLA Ops:
  7.2 2.3 collective-permute-start.1
  10.7 1.0 scatter_custom_fusion
  11.7 0.7 select_reduce_fusion
  12.4 15.4 %collective-permute-done.1 = bf16[128,6144]{1,0:T(8,128)(2,1)} collective-permute-done((bf16[128,6144]{1,0:T(8,128)(2,1)}, bf16[128,6144]{1,0:T(8,128)(2,1)}, u32[]{:S(2)}, u32[]{:S(2)}) %collective-permute-start.1) | collective-permute-done | bytes 1572896 | tf_op jit(solution)/shard_map/ppermute | solution.py:12
  27.8 1.8 multiply_convert_fusion
  29.5 1.6 gather_fusion.2
  31.2 0.8 gather_fusion
  32.2 1.1 broadcast_select_fusion
  34.1 70.5 %all-gather.3.cloned.1.call-done = bf16[640,6144]{1,0:T(8,128)(2,1)} async-done(((bf16[40,6144]{1,0:T(8,128)(2,1)}), bf16[640,6144]{1,0:T(8,128)(2,1)}) %all-gather.3.cloned.1.call-update) | async-done | bytes 7864336 | tf_op jit(solution)/shard_map/all_gather | solution.py:55
  104.6 8.5 %fusion.8 = f32[640,512]{1,0:T(8,128)S(1)} fusion(bf16[640,6144]{1,0:T(8,128)(2,1)} %all-gather.3.cloned.1.call-done, bf16[1,6144,512]{2,1,0:T(8,128)(2,1)} %param.11), kind=kOutput, calls=%fused_computation.15 | convolution fusion | flops 4026531840 | bytes 15466496 | tf_op jit(solution)/shard_map/dot_general | solution.py:58
  113.1 6.4 %fusion.4 = f32[640,512]{1,0:T(8,128)S(1)} fusion(bf16[640,6144]{1,0:T(8,128)(2,1)S(1)} %copy-done.2, bf16[1,6144,512]{2,1,0:T(8,128)(2,1)} %param.12), kind=kOutput, calls=%fused_computation.11 | convolution fusion | flops 4026531840 | bytes 15466496 | tf_op jit(solution)/shard_map/dot_general | solution.py:59
  119.6 56.0 %all-gather.5.cloned.1.call-done = bf16[640,6144]{1,0:T(8,128)(2,1)} async-done(((bf16[40,6144]{1,0:T(8,128)(2,1)}), bf16[640,6144]{1,0:T(8,128)(2,1)}) %all-gather.5.cloned.1.call-update) | async-done | bytes 7864336 | tf_op jit(solution)/shard_map/all_gather | solution.py:75
  175.6 8.5 %fusion = f32[640,512]{1,0:T(8,128)S(1)} fusion(bf16[640,6144]{1,0:T(8,128)(2,1)} %all-gather.5.cloned.1.call-done, bf16[1,512,6144]{2,1,0:T(8,128)(2,1)} %param.13), kind=kOutput, calls=%fused_computation.7 | convolution fusion | flops 4026531840 | bytes 15466496 | tf_op jit(solution)/shard_map/dot_general | solution.py:78
  184.0 1.0 copy-done.1
  185.1 10.6 %fusion.6 = f32[640,6144]{1,0:T(8,128)} fusion(bf16[1,6144,512]{2,1,0:T(8,128)(2,1)} %param.11, f32[640,512]{1,0:T(8,128)S(1)} %fusion.8, f32[640,512]{1,0:T(8,128)S(1)} %fusion, f32[640,512]{1,0:T(8,128)S(1)} %fusion.4), kind=kOutput, calls=%fused_computation.13 | convolution fusion | flops 4029808640 | bytes 25952256 | tf_op jit(solution)/shard_map/dot_general | solution.py:88
  195.7 15.1 %add_convert_fusion = bf16[640,6144]{1,0:T(8,128)(2,1)} fusion(f32[640,6144]{1,0:T(8,128)} %fusion.6, bf16[1,6144,512]{2,1,0:T(8,128)(2,1)} %param.12, f32[640,512]{1,0:T(8,128)} %copy-done.1, f32[640,512]{1,0:T(8,128)S(1)} %fusion.8), kind=kOutput, calls=%fused_computation.5 | convolution fusion | flops 4036362240 | bytes 32505856 | tf_op jit(solution)/shard_map/dot_general | solution.py:89
  211.0 9.2 %convolution_convert_fusion = bf16[640,6144]{1,0:T(8,128)(2,1)} fusion(bf16[1,512,6144]{2,1,0:T(8,128)(2,1)} %param.13, f32[640,512]{1,0:T(8,128)S(1)} %fusion.4, f32[640,512]{1,0:T(8,128)S(1)} %fusion.8), kind=kOutput, calls=%fused_computation.6 | convolution fusion | flops 4032430080 | bytes 16777216 | tf_op jit(solution)/shard_map/dot_general | solution.py:66
  220.2 75.0 %reduce-scatter.9.cloned.1.call-done = bf16[40,6144]{1,0:T(8,128)(2,1)} async-done(((bf16[640,6144]{1,0:T(8,128)(2,1)}), bf16[40,6144]{1,0:T(8,128)(2,1)}) %reduce-scatter.9.cloned.1.call-update) | async-done | bytes 491536
  295.2 4.1 %gather_fusion.3 = bf16[128,6144]{1,0:T(8,128)(2,1)S(1)} fusion(bf16[40,6144]{1,0:T(8,128)(2,1)} %reduce-scatter.9.cloned.1.call-done, s32[1024]{0:T(1024)S(1)} %pad_clamp_fusion), kind=kCustom, calls=%fused_computation.3 | custom fusion | bytes 3146240 | tf_op jit(solution)/shard_map/gather | solution.py:94
  299.3 1.5 fusion.10
  300.8 81.9 %reduce-scatter.7.cloned.1.call-done = bf16[40,6144]{1,0:T(8,128)(2,1)} async-done(((bf16[640,6144]{1,0:T(8,128)(2,1)}), bf16[40,6144]{1,0:T(8,128)(2,1)}) %reduce-scatter.7.cloned.1.call-update) | async-done | bytes 491536
  382.7 1.1 convert_element_type.68
  383.8 3.2 gather_fusion.1
  387.0 3.4 fusion.12
  (25 shorter events, 2.4 us)
Async XLA Ops:
  7.2 97.4 %all-gather.3.cloned.1.call-start = ((), (), s32[]{:S(2)}) async-start(), calls=%async_computation.2 | async-start | bytes 8355840 | tf_op jit(solution)/shard_map/all_gather | solution.py:55
  7.2 20.6 %collective-permute-start.1 = (bf16[128,6144]{1,0:T(8,128)(2,1)}, bf16[128,6144]{1,0:T(8,128)(2,1)}, u32[]{:S(2)}, u32[]{:S(2)}) collective-permute-start(bf16[128,6144]{1,0:T(8,128)(2,1)} %bitcast.33), channel_id=1, source_target_pairs={{0,112},{16,0},{32,16},{48,32},{64,48},{80,64},{96,80},{112,96},{1... | collective-permute-start | bytes 4718600 | tf_op jit(solution)/shard_map/ppermute | solution.py:12
  9.5 21.6 %collective-permute-start = (bf16[128,6144]{1,0:T(8,128)(2,1)}, bf16[128,6144]{1,0:T(8,128)(2,1)S(1)}, u32[]{:S(2)}, u32[]{:S(2)}) collective-permute-start(bf16[128,6144]{1,0:T(8,128)(2,1)} %bitcast.34), channel_id=1, source_target_pairs={{0,16},{16,32},{32,48},{48,64},{64,80},{80,96},{96,112},{112,0},{1... | collective-permute-start | bytes 4718600 | tf_op jit(solution)/shard_map/ppermute | solution.py:12
  31.2 1.0 copy-start
  33.3 142.3 %all-gather.5.cloned.1.call-start = ((), (), s32[]{:S(2)}) async-start(), calls=%async_computation.3 | async-start | bytes 8355840 | tf_op jit(solution)/shard_map/all_gather | solution.py:75
  34.1 261.1 %reduce-scatter.9.cloned.1.call-start = ((), (), s32[]{:S(2)}) async-start(), calls=%async_computation.5 | async-start | bytes 8355840
  104.6 8.5 %copy-start.2 = (bf16[640,6144]{1,0:T(8,128)(2,1)S(1)}, bf16[640,6144]{1,0:T(8,128)(2,1)}, u32[]{:S(2)}) copy-start(bf16[640,6144]{1,0:T(8,128)(2,1)} %all-gather.3.cloned.1.call-done) | copy-start | bytes 23592964
  184.0 1.1 copy-start.1
  210.8 171.9 %reduce-scatter.7.cloned.1.call-start = ((), (), s32[]{:S(2)}) async-start(), calls=%async_computation.4 | async-start | bytes 8355840
Sparse Core Ops, SparseCore 0:
  33.4 71.1 all-gather.2
  107.3 68.1 all-gather.4
  210.9 84.2 reduce-scatter.8
  298.6 84.0 reduce-scatter.6
where the time goes:
time: 397 us
  waiting for transfers between devices  299 us (75%)
  matrix products  58.3 us (15%)
  between operations  13.9 us (4%)
  local copies, waits for them, and re-layouts  12.1 us (3%)
  other arithmetic  10.6 us (3%)
    unnamed x6, waiting for transfers between devices  158 us
    all_gather x1, waiting for transfers between devices, body(): all_acts = lax.all_gather(slot_acts, 'expert', axis=0, tiled=True)  70.5 us
    all_gather x1, waiting for transfers between devices, body(): all_grads = lax.all_gather(slot_grads, 'expert', axis=0, tiled=True)  56 us
    ppermute x2, waiting for transfers between devices, shifted(): return lax.ppermute(value, axis, pairs)  15.4 us
    dot_general x1, matrix products, backward_term(): lax.dot_general(up_grad, up_cols, contract, preferred_element_type=jnp.fl...  15.1 us
    dot_general x1, matrix products, backward_term(): lax.dot_general(gate_grad, gate_cols, contract, preferred_element_type=jn...  10.6 us
    dot_general x1, matrix products, forward_term(): return jnp.dot(hidden, down_rows, preferred_element_type=jnp.float32)  9.21 us
    dot_general x1, matrix products, forward_rows(): pre_gate = jnp.dot(rows_in, gate_cols, preferred_element_type=jnp.float32)  8.51 us
  transfers between devices with their start and end apart: 6, of which 5 were waited for; matrix products, arithmetic and copies ran while one was open for 9% of the time, Pallas kernels for 0%

commit v1 on v0

v1 whole, which is shorter than its diff:
```python
import functools

import jax
import jax.numpy as jnp
from jax import lax
from jax.experimental import pallas as pl
from jax.experimental.pallas import tpu as pltpu
from jax.sharding import PartitionSpec as P

CAP = 40
SIDE = 4
MESH = pl.DeviceIdType.MESH
F32 = jnp.float32
BF16 = jnp.bfloat16
HALVES = (0, 1)
PIECES = (0, 1)
CORNERS = ((0, 0), (1, 0), (0, 1), (1, 1))


def dot_nn(lhs, rhs):
    return lax.dot_general(lhs, rhs, (((1,), (0,)), ((), ())), preferred_element_type=F32)


def dot_nt(lhs, rhs):
    return lax.dot_general(lhs, rhs, (((1,), (1,)), ((), ())), preferred_element_type=F32)


class Place:
    def __init__(self, sections):
        self.sections = sections
        self.section = lax.axis_index("section")
        self.expert = lax.axis_index("expert")
        self.at = (self.expert // SIDE, self.expert % SIDE)

    def axis(self, half, phase):
        return 1 - half if phase == 1 else half

    def beside(self, axis, step):
        z, y = self.at
        if axis == 0:
            z = (z + step) % SIDE
        else:
            y = (y + step) % SIDE
        return (self.section, z * SIDE + y)

    def other_section(self, step):
        return ((self.section + step) % self.sections, self.expert)

    def outer(self, half):
        return self.at[half]

    def inner(self, half):
        return self.at[1 - half]


class Links:
    def __init__(self, send_sem, recv_sem):
        self.send_sem, self.recv_sem = send_sem, recv_sem
        self.used = 0

    def copy(self, src, dst, device):
        k = self.used
        self.used += 1
        return pltpu.make_async_remote_copy(
            src_ref=src,
            dst_ref=dst,
            send_sem=self.send_sem.at[k],
            recv_sem=self.recv_sem.at[k],
            device_id=device,
            device_id_type=MESH,
        )


class GatherRing:
    def __init__(self, place, links, half, phase, piece):
        axis = place.axis(half, phase)
        me = place.at[axis]
        plus, minus = place.beside(axis, 1), place.beside(axis, SIDE - 1)
        before, after = (me + SIDE - 1) % SIDE, (me + 1) % SIDE
        self.own = [
            [links.copy(piece(q, me), piece(q, me), device) for device in (plus, minus)]
            for q in PIECES
        ]
        self.passed = [
            links.copy(piece(0, before), piece(0, before), plus),
            links.copy(piece(1, after), piece(1, after), minus),
        ]

    def start(self, q):
        self.own[q][q].start()
        self.own[q][1 - q].start()

    def relay(self):
        for q in PIECES:
            self.own[q][q].wait_recv()
            self.passed[q].start()

    def finish(self):
        self.own[0][1].wait_recv()
        self.own[1][0].wait_recv()
        self.passed[0].wait_recv()
        self.passed[1].wait_recv()

    def wait_sends(self):
        for q in PIECES:
            for way in (0, 1):
                self.own[q][way].wait_send()
            self.passed[q].wait_send()


class ReduceRing:
    def __init__(self, place, links, half, phase, piece, through, landed):
        axis = place.axis(half, phase)
        me = place.at[axis]
        plus, minus = place.beside(axis, 1), place.beside(axis, SIDE - 1)
        before, after = (me + SIDE - 1) % SIDE, (me + 1) % SIDE
        opposite = (me + 2) % SIDE
        self.piece, self.me, self.through, self.landed = piece, me, through, landed
        self.next = (after, before)
        devices = (plus, minus)
        self.far = [links.copy(piece(q, opposite), through(q), devices[q]) for q in PIECES]
        self.near = [
            links.copy(piece(1 - q, self.next[q]), landed(q, 1 - q), devices[q]) for q in PIECES
        ]
        self.passed = [links.copy(through(q), landed(q, q), devices[q]) for q in PIECES]

    def start(self):
        for q in PIECES:
            self.far[q].start()
        for q in PIECES:
            self.near[q].start()

    def relay(self, add_into):
        for q in PIECES:
            self.far[q].wait_recv()
            add_into(self.through(q), self.piece(q, self.next[q]))
        for q in PIECES:
            self.passed[q].start()

    def finish(self):
        for q in PIECES:
            self.near[q].wait_recv()
            self.passed[q].wait_recv()

    def wait_sends(self):
        for q in PIECES:
            self.far[q].wait_send()
            self.near[q].wait_send()
            self.passed[q].wait_send()


def kernel(
    sections,
    acts_ref,
    cots_ref,
    ids_ref,
    probs_ref,
    gate_ref,
    up_ref,
    down_ref,
    out_ref,
    grad_ref,
    gate_w,
    up_w,
    down_w,
    info,
    rows_x,
    rows_g,
    part,
    pre_g,
    pre_u,
    hid,
    grad_g,
    grad_u,
    thru_big,
    land_big,
    thru_small,
    land_small,
    send_sem,
    recv_sem,
    load_sem,
    store_sem,
):
    place = Place(sections)
    links = Links(send_sem, recv_sem)
    toks, width = acts_ref.shape
    cols = width // 4
    units = gate_ref.shape[1]
    group = SIDE * CAP

    def span(h, q):
        return pl.ds((h * 2 + q) * cols, cols)

    barrier = pltpu.get_barrier_semaphore()
    around = [place.beside(axis, step) for axis in (0, 1) for step in (1, SIDE - 1)]
    around += [place.other_section(step) for step in (1, sections - 1)]
    for device in around:
        pl.semaphore_signal(barrier, inc=1, device_id=device, device_id_type=MESH)

    acts_here = down_w.at[pl.ds(0, toks)]
    cots_here = down_w.at[pl.ds(toks, toks)]
    load_acts = pltpu.make_async_copy(acts_ref, acts_here, load_sem.at[0])
    load_cots = pltpu.make_async_copy(cots_ref, cots_here, load_sem.at[1])
    load_gate = pltpu.make_async_copy(gate_ref, gate_w, load_sem.at[2])
    load_up = pltpu.make_async_copy(up_ref, up_w, load_sem.at[3])
    load_down = pltpu.make_async_copy(down_ref, down_w, load_sem.at[4])
    load_acts.start()
    load_cots.start()

    chosen = ids_ref[...] == 0
    flags = jnp.where(chosen, 1.0, 0.0).astype(F32)
    weights = jnp.where(chosen, probs_ref[...], 0.0)
    picked = jnp.broadcast_to(flags[0:1] + flags[1:2], (8, toks))
    share = jnp.broadcast_to(weights[0:1] + weights[1:2], (8, toks))
    earlier = lax.broadcasted_iota(jnp.int32, (toks, toks), 0) < lax.broadcasted_iota(
        jnp.int32, (toks, toks), 1
    )
    rank = dot_nn(picked.astype(BF16), jnp.where(earlier, 1.0, 0.0).astype(BF16))
    slot = jnp.where(picked > 0.5, rank, -1.0)
    line = lax.broadcasted_iota(jnp.int32, (8, toks), 0)
    info[0] = jnp.where(line == 0, slot, share)

    pl.semaphore_wait(barrier, len(around))
    info_back = links.copy(info.at[0], info.at[1], place.other_section(sections - 1))
    info_on = links.copy(info.at[0], info.at[2], place.other_section(1))
    info_back.start()
    info_on.start()

    def selection(block):
        slot_line = block[0:1, :]
        share_line = block[1:2, :]
        number = lax.broadcasted_iota(jnp.int32, (CAP, toks), 0).astype(F32)
        hit = number == slot_line
        pick = jnp.where(hit, 1.0, 0.0).astype(BF16)
        slot_share = jnp.sum(jnp.where(hit, share_line, 0.0), axis=1, keepdims=True)
        return pick, slot_share

    def own_slot(rows, h, q):
        return rows.at[h, q, place.outer(h), place.inner(h)]

    load_acts.wait()
    info_back.wait_recv()
    pick, _ = selection(info[1])
    send_x = {}
    for h, q in CORNERS:
        part[h, q, 0, 0] = dot_nn(pick, down_w[pl.ds(0, toks), span(h, q)]).astype(BF16)
        send_x[h, q] = links.copy(
            part.at[h, q, 0, 0], own_slot(rows_x, h, q), place.other_section(1)
        )
        send_x[h, q].start()

    load_cots.wait()
    info_on.wait_recv()
    pick, slot_share = selection(info[2])
    send_g = {}
    for h, q in CORNERS:
        chosen_rows = dot_nn(pick, down_w[pl.ds(toks, toks), span(h, q)])
        part[h, q, 0, 1] = (chosen_rows * slot_share).astype(BF16)
        send_g[h, q] = links.copy(
            part.at[h, q, 0, 1], own_slot(rows_g, h, q), place.other_section(sections - 1)
        )
        send_g[h, q].start()

    load_gate.start()
    load_up.start()
    load_down.start()

    def gathers(rows):
        first = [
            GatherRing(place, links, h, 1, lambda q, j, h=h: rows.at[h, q, place.outer(h), j])
            for h in HALVES
        ]
        second = [
            GatherRing(place, links, h, 2, lambda q, j, h=h: rows.at[h, q, j]) for h in HALVES
        ]
        return first, second

    first_x, second_x = gathers(rows_x)
    first_g, second_g = gathers(rows_g)

    for h, q in CORNERS:
        send_x[h, q].wait_recv()
        first_x[h].start(q)
    for h, q in CORNERS:
        send_g[h, q].wait_recv()
        first_g[h].start(q)
    for h in HALVES:
        first_x[h].relay()
    for h in HALVES:
        first_x[h].finish()
        for q in PIECES:
            second_x[h].start(q)
    for h in HALVES:
        first_g[h].relay()
    for h in HALVES:
        first_g[h].finish()
        for q in PIECES:
            second_g[h].start(q)
    for h in HALVES:
        second_x[h].relay()
    for h in HALVES:
        second_x[h].finish()

    def block_rows(rows, h, q, z):
        value = rows[h, q, z] if h == 0 else rows[h, q, :, z]
        return value.reshape(group, cols)

    def put_rows(rows, h, q, z, value):
        value = value.astype(BF16).reshape(SIDE, CAP, cols)
        if h == 0:
            rows[h, q, z] = value
        else:
            rows[h, q, :, z] = value

    load_gate.wait()
    load_up.wait()

    def project(z, carry):
        here = pl.ds(pl.multiple_of(z * group, group), group)
        total_g = jnp.zeros((group, units), F32)
        total_u = jnp.zeros((group, units), F32)
        for h, q in CORNERS:
            block = block_rows(rows_x, h, q, z)
            total_g += dot_nn(block, gate_w[span(h, q), :])
            total_u += dot_nn(block, up_w[span(h, q), :])
        pre_g[here, :] = total_g
        pre_u[here, :] = total_u
        hid[here, :] = (total_g * jax.nn.sigmoid(total_g) * total_u).astype(BF16)
        return carry

    lax.fori_loop(0, SIDE, project, 0)

    for h in HALVES:
        second_g[h].relay()

    load_down.wait()
    for h, q in CORNERS:
        send_x[h, q].wait_send()
        send_g[h, q].wait_send()

    def forward_terms(z, carry):
        here = pl.ds(pl.multiple_of(z * group, group), group)
        units_here = hid[here, :]
        for h, q in CORNERS:
            put_rows(part, h, q, z, dot_nn(units_here, down_w[:, span(h, q)]))
        return carry

    lax.fori_loop(0, SIDE, forward_terms, 0)

    def reduces(rows, which):
        first = [
            ReduceRing(
                place,
                links,
                h,
                2,
                lambda q, j, h=h: rows.at[h, q, j],
                lambda q, h=h: thru_big.at[which, h, q],
                lambda way, q, h=h: land_big.at[which, h, way, q],
            )
            for h in HALVES
        ]
        second = [
            ReduceRing(
                place,
                links,
                h,
                1,
                lambda q, j, h=h: rows.at[h, q, place.outer(h), j],
                lambda q, h=h: thru_small.at[which, h, q],
                lambda way, q, h=h: land_small.at[which, h, way, q],
            )
            for h in HALVES
        ]
        return first, second

    def add_big(into, term):
        def step(j, carry):
            into[j] = (into[j].astype(F32) + term[j].astype(F32)).astype(BF16)
            return carry

        lax.fori_loop(0, SIDE, step, 0)

    def add_small(into, term):
        into[...] = (into[...].astype(F32) + term[...].astype(F32)).astype(BF16)

    def close_first(rows, which, h):
        mine = place.outer(h)

        def step(j, carry):
            for q in PIECES:
                total = rows[h, q, mine, j].astype(F32)
                for way in (0, 1):
                    total += land_big[which, h, way, q, j].astype(F32)
                rows[h, q, mine, j] = total.astype(BF16)
            return carry

        lax.fori_loop(0, SIDE, step, 0)

    first_o, second_o = reduces(part, 0)
    first_b, second_b = reduces(rows_x, 1)

    for h in HALVES:
        first_o[h].start()

    for h in HALVES:
        second_g[h].finish()

    def unit_grads(z, carry):
        here = pl.ds(pl.multiple_of(z * group, group), group)
        hidden_grad = jnp.zeros((group, units), F32)
        for h, q in CORNERS:
            hidden_grad += dot_nt(block_rows(rows_g, h, q, z), down_w[:, span(h, q)])
        gate = pre_g[here, :]
        sigma = jax.nn.sigmoid(gate)
        grad_g[here, :] = (
            hidden_grad * pre_u[here, :] * (sigma * (1.0 + gate * (1.0 - sigma)))
        ).astype(BF16)
        grad_u[here, :] = (hidden_grad * (gate * sigma)).astype(BF16)
        return carry

    lax.fori_loop(0, SIDE, unit_grads, 0)

    for h in HALVES:
        first_o[h].relay(add_big)

    for rings in (first_x, second_x):
        for h in HALVES:
            rings[h].wait_sends()

    def backward_terms(z, carry):
        here = pl.ds(pl.multiple_of(z * group, group), group)
        gate_here, up_here = grad_g[here, :], grad_u[here, :]
        for h, q in CORNERS:
            term = dot_nt(gate_here, gate_w[span(h, q), :])
            put_rows(rows_x, h, q, z, term + dot_nt(up_here, up_w[span(h, q), :]))
        return carry

    lax.fori_loop(0, SIDE, backward_terms, 0)

    for h in HALVES:
        first_b[h].start()

    local_pick, local_share = selection(info[0])

    def close_second(rows, which, h, q, staged):
        total = rows[h, q, place.outer(h), place.inner(h)].astype(F32)
        for way in (0, 1):
            total += land_small[which, h, way, q].astype(F32)
        if which == 0:
            total = total * local_share
        spread = lax.dot_general(
            local_pick, total.astype(BF16), (((0,), (0,)), ((), ())), preferred_element_type=F32
        )
        down_w[pl.ds(staged, toks), span(h, q)] = spread.astype(BF16)

    def close(rows, which, first, second):
        staged = which * toks
        for h in HALVES:
            second[h].relay(add_small)
        for h in HALVES:
            second[h].finish()
            for q in PIECES:
                close_second(rows, which, h, q, staged)

    for h in HALVES:
        first_o[h].finish()
        close_first(part, 0, h)
        second_o[h].start()
    for h in HALVES:
        first_b[h].relay(add_big)
    close(part, 0, first_o, second_o)
    store_out = pltpu.make_async_copy(acts_here, out_ref, store_sem.at[0])
    store_out.start()
    for h in HALVES:
        first_b[h].finish()
        close_first(rows_x, 1, h)
        second_b[h].start()
    close(rows_x, 1, first_b, second_b)
    store_grad = pltpu.make_async_copy(cots_here, grad_ref, store_sem.at[1])
    store_grad.start()

    info_back.wait_send()
    info_on.wait_send()
    for rings in (first_g, second_g, first_o, second_o, first_b, second_b):
        for h in HALVES:
            rings[h].wait_sends()
    store_out.wait()
    store_grad.wait()
    assert links.used == COPIES


COPIES = 2 + 8 + 2 * 4 * 6 + 2 * 4 * 6


def body(sections, sent_acts, sent_cots, expert_ids, gate_probs, gate_weight, up_weight, down_weight):
    acts, cots = sent_acts[0], sent_cots[0]
    ids, probs = expert_ids[0].T, gate_probs[0].T
    toks, width = acts.shape
    cols = width // 4
    units = gate_weight.shape[2]
    rows = SIDE * SIDE * CAP
    hbm = pl.BlockSpec(memory_space=pl.ANY)
    vmem = pl.BlockSpec(memory_space=pltpu.VMEM)
    block = (CAP, cols)
    out_acts, in_grads = pl.pallas_call(
        functools.partial(kernel, sections),
        out_shape=(
            jax.ShapeDtypeStruct((toks, width), BF16),
            jax.ShapeDtypeStruct((toks, width), BF16),
        ),
        in_specs=[hbm, hbm, vmem, vmem, hbm, hbm, hbm],
        out_specs=(hbm, hbm),
        scratch_shapes=[
            pltpu.VMEM((width, units), BF16),
            pltpu.VMEM((width, units), BF16),
            pltpu.VMEM((units, width), BF16),
            pltpu.VMEM((3, 8, toks), F32),
            pltpu.VMEM((2, 2, SIDE, SIDE) + block, BF16),
            pltpu.VMEM((2, 2, SIDE, SIDE) + block, BF16),
            pltpu.VMEM((2, 2, SIDE, SIDE) + block, BF16),
            pltpu.VMEM((rows, units), F32),
            pltpu.VMEM((rows, units), F32),
            pltpu.VMEM((rows, units), BF16),
            pltpu.VMEM((rows, units), BF16),
            pltpu.VMEM((rows, units), BF16),
            pltpu.VMEM((2, 2, 2, SIDE) + block, BF16),
            pltpu.VMEM((2, 2, 2, 2, SIDE) + block, BF16),
            pltpu.VMEM((2, 2, 2) + block, BF16),
            pltpu.VMEM((2, 2, 2, 2) + block, BF16),
            pltpu.SemaphoreType.DMA((COPIES,)),
            pltpu.SemaphoreType.DMA((COPIES,)),
            pltpu.SemaphoreType.DMA((5,)),
            pltpu.SemaphoreType.DMA((2,)),
        ],
        compiler_params=pltpu.CompilerParams(
            collective_id=0, has_side_effects=True, vmem_limit_bytes=67043328
        ),
    )(acts, cots, ids, probs, gate_weight[0], up_weight[0], down_weight[0])
    return (out_acts[None], in_grads[None])


def solution(mesh):
    placed = (
        P("section", "expert", None),
        P("section", "expert", None),
        P("section", "expert", None),
        P("section", "expert", None),
        P("section", None, "expert"),
        P("section", None, "expert"),
        P("section", "expert", None),
    )
    return jax.shard_map(
        functools.partial(body, mesh.shape["section"]),
        mesh=mesh,
        in_specs=placed,
        out_specs=(P("section", "expert", None), P("section", "expert", None)),
        check_vma=False,
    )
```

time: 397 us -> 192 us (0.48)
  waiting for transfers between devices: 299 us -> 0 us
  Pallas kernels: 0 us -> 187 us
  matrix products: 58.3 us -> 0 us
  between operations: 13.9 us -> 0.65 us
  other arithmetic: 10.6 us -> 0 us
  local copies, waits for them, and re-layouts: 12.1 us -> 3.95 us
    pallas_call x0 -> x1, Pallas kernels: none -> 187 us  [body(): pl.pallas_call(functools.partial(kernel, sections), out_shape=(jax.ShapeD...]
    unnamed x6 -> x0, waiting for transfers between devices: 158 us -> none
    all_gather x2 -> x0, waiting for transfers between devices: 126 us -> none  [the longest x1 70.5 us: body(): all_acts = lax.all_gather(slot_acts, 'expert', axis=0, tiled=True)]
    dot_general x6 -> x0, matrix products: 58.3 us -> none  [the longest x1 15.1 us: backward_term(): lax.dot_general(up_grad, up_cols, contract, preferred_element_type=jnp.fl...]
    ppermute x2 -> x0, waiting for transfers between devices: 15.4 us -> none  [shifted(): return lax.ppermute(value, axis, pairs)]
    gather x4 -> x0, local copies, waits for them, and re-layouts: 9.74 us -> none  [the longest x1 4.09 us: body(): slot_back[back_index]]
    convert_element_type x5 -> x0, other arithmetic: 7.79 us -> none  [the longest x1 3.43 us: body(): jnp.where(picked[:, None], share[:, None] * slot_out[back_index], 0.0)]
  transfers between devices with their start and end apart: 6 -> 0, of which waited for: 5 -> 0; matrix products, arithmetic and copies ran while one was open for 9% -> 0% of each run, Pallas kernels for 0% -> 0%
where the time goes in v1:
time: 192 us
  Pallas kernels  187 us (97%)
  local copies, waits for them, and re-layouts  3.95 us (2%)
    pallas_call x1, Pallas kernels, body(): pl.pallas_call(functools.partial(kernel, sections), out_shape=(jax.ShapeD...  187 us
    unnamed x4, local copies, waits for them, and re-layouts  3.95 us

profile of v1, /device:TPU:0, one launch (start us, length us, event | category | flops | bytes accessed | tf_op | source)
XLA Modules:
  0.0 191.5 jit_solution(12015211317106489725)
XLA Ops:
  0.6 186.9 %shard_map.86 = (bf16[128,6144]{1,0:T(8,128)(2,1)}, bf16[128,6144]{1,0:T(8,128)(2,1)}) custom-call(bf16[128,6144]{1,0:T(8,128)(2,1)} %bitcast.16, bf16[128,6144]{1,0:T(8,128)(2,1)} %bitcast.17, s32[2,128]{1,0:T(2,128)} %bitcast.20, f32[2,128]{1,0:T(2,128)} %bitcast.21, bf16[6144,512]{1,0:T(8,128)(2,1)} %bitcast.13, bf16[6144,512]{1,0:T(8,128)(2,1)} %bitcast.14, ...), custom_call_target="tpu_custom_call" | custom-call | tf_op jit(solution)/shard_map/pallas_call | solution.py:506
  187.6 0.0 copy-start
  187.6 2.8 %copy.11 = bf16[1,128,6144]{2,1,0:T(8,128)(2,1)} copy(bf16[1,128,6144]{2,1,0:T(8,128)(2,1)} %bitcast.19) | data formatting | bytes 3145728
  190.4 0.0 copy-done
  190.4 1.1 copy.12
Async XLA Ops:
  187.6 2.8 %copy-start = (bf16[128,6144]{1,0:T(8,128)(2,1)S(1)}, bf16[128,6144]{1,0:T(8,128)(2,1)}, u32[]{:S(2)}) copy-start(bf16[128,6144]{1,0:T(8,128)(2,1)} %get-tuple-element.5) | copy-start | bytes 4718596

commit v2 on v1

--- a/solution.py
+++ b/solution.py
@@ -124,11 +124,17 @@
         ]
         self.passed = [links.copy(through(q), landed(q, q), devices[q]) for q in PIECES]
 
+    def start_far(self):
+        for q in PIECES:
+            self.far[q].start()
+
+    def start_near(self):
+        for q in PIECES:
+            self.near[q].start()
+
     def start(self):
-        for q in PIECES:
-            self.far[q].start()
-        for q in PIECES:
-            self.near[q].start()
+        self.start_far()
+        self.start_near()
 
     def relay(self, add_into):
         for q in PIECES:
@@ -293,11 +299,11 @@
     for h in HALVES:
         first_g[h].relay()
     for h in HALVES:
+        second_x[h].relay()
+    for h in HALVES:
         first_g[h].finish()
         for q in PIECES:
             second_g[h].start(q)
-    for h in HALVES:
-        second_x[h].relay()
     for h in HALVES:
         second_x[h].finish()
 
@@ -439,7 +445,7 @@
     lax.fori_loop(0, SIDE, backward_terms, 0)
 
     for h in HALVES:
-        first_b[h].start()
+        first_b[h].start_far()
 
     local_pick, local_share = selection(info[0])
 
@@ -454,29 +460,32 @@
         )
         down_w[pl.ds(staged, toks), span(h, q)] = spread.astype(BF16)
 
-    def close(rows, which, first, second):
-        staged = which * toks
-        for h in HALVES:
-            second[h].relay(add_small)
+    def close(rows, which, second):
         for h in HALVES:
             second[h].finish()
             for q in PIECES:
-                close_second(rows, which, h, q, staged)
+                close_second(rows, which, h, q, which * toks)
 
     for h in HALVES:
         first_o[h].finish()
         close_first(part, 0, h)
         second_o[h].start()
     for h in HALVES:
+        first_b[h].start_near()
+    for h in HALVES:
         first_b[h].relay(add_big)
-    close(part, 0, first_o, second_o)
+    for h in HALVES:
+        second_o[h].relay(add_small)
+    close(part, 0, second_o)
     store_out = pltpu.make_async_copy(acts_here, out_ref, store_sem.at[0])
     store_out.start()
     for h in HALVES:
         first_b[h].finish()
         close_first(rows_x, 1, h)
         second_b[h].start()
-    close(rows_x, 1, first_b, second_b)
+    for h in HALVES:
+        second_b[h].relay(add_small)
+    close(rows_x, 1, second_b)
     store_grad = pltpu.make_async_copy(cots_here, grad_ref, store_sem.at[1])
     store_grad.start()
 

time: 192 us -> 184 us (0.958)
  Pallas kernels: 187 us -> 179 us
    pallas_call x1, Pallas kernels: 187 us -> 179 us  [body(): pl.pallas_call(functools.partial(kernel, sections), out_shape=(jax.ShapeD...]
where the time goes in v2:
time: 184 us; the launch traced here: 183 us
  Pallas kernels  179 us (97%)
  local copies, waits for them, and re-layouts  3.95 us (2%)
    pallas_call x1, Pallas kernels, body(): pl.pallas_call(functools.partial(kernel, sections), out_shape=(jax.ShapeD...  179 us
    unnamed x4, local copies, waits for them, and re-layouts  3.95 us

profile of v2, /device:TPU:0, one launch (start us, length us, event | category | flops | bytes accessed | tf_op | source)
XLA Modules:
  0.0 183.4 jit_solution(10243162922286037677)
XLA Ops:
  0.6 178.8 %shard_map.86 = (bf16[128,6144]{1,0:T(8,128)(2,1)}, bf16[128,6144]{1,0:T(8,128)(2,1)}) custom-call(bf16[128,6144]{1,0:T(8,128)(2,1)} %bitcast.16, bf16[128,6144]{1,0:T(8,128)(2,1)} %bitcast.17, s32[2,128]{1,0:T(2,128)} %bitcast.20, f32[2,128]{1,0:T(2,128)} %bitcast.21, bf16[6144,512]{1,0:T(8,128)(2,1)} %bitcast.13, bf16[6144,512]{1,0:T(8,128)(2,1)} %bitcast.14, ...), custom_call_target="tpu_custom_call" | custom-call | tf_op jit(solution)/shard_map/pallas_call | solution.py:515
  179.4 0.0 copy-start
  179.4 2.8 %copy.11 = bf16[1,128,6144]{2,1,0:T(8,128)(2,1)} copy(bf16[1,128,6144]{2,1,0:T(8,128)(2,1)} %bitcast.19) | data formatting | bytes 3145728
  182.2 0.0 copy-done
  182.2 1.1 copy.12
Async XLA Ops:
  179.4 2.8 %copy-start = (bf16[128,6144]{1,0:T(8,128)(2,1)S(1)}, bf16[128,6144]{1,0:T(8,128)(2,1)}, u32[]{:S(2)}) copy-start(bf16[128,6144]{1,0:T(8,128)(2,1)} %get-tuple-element.5) | copy-start | bytes 4718596

commit v3 on v2

--- a/solution.py
+++ b/solution.py
@@ -23,6 +23,32 @@
 
 def dot_nt(lhs, rhs):
     return lax.dot_general(lhs, rhs, (((1,), (1,)), ((), ())), preferred_element_type=F32)
+
+
+def routing(ids, probs):
+    toks = ids.shape[1]
+    chosen = ids == 0
+    flags = jnp.where(chosen, 1.0, 0.0).astype(F32)
+    weights = jnp.where(chosen, probs, 0.0)
+    picked = jnp.broadcast_to(flags[0:1] + flags[1:2], (8, toks))
+    share = jnp.broadcast_to(weights[0:1] + weights[1:2], (8, toks))
+    earlier = lax.broadcasted_iota(jnp.int32, (toks, toks), 0) < lax.broadcasted_iota(
+        jnp.int32, (toks, toks), 1
+    )
+    rank = dot_nn(picked.astype(BF16), jnp.where(earlier, 1.0, 0.0).astype(BF16))
+    slot = jnp.where(picked > 0.5, rank, -1.0)
+    line = lax.broadcasted_iota(jnp.int32, (8, toks), 0)
+    return jnp.where(line == 0, slot, share)
+
+
+def selection(toks, block):
+    slot_line = block[0:1, :]
+    share_line = block[1:2, :]
+    number = lax.broadcasted_iota(jnp.int32, (CAP, toks), 0).astype(F32)
+    hit = number == slot_line
+    pick = jnp.where(hit, 1.0, 0.0).astype(BF16)
+    slot_share = jnp.sum(jnp.where(hit, share_line, 0.0), axis=1, keepdims=True)
+    return pick, slot_share
 
 
 class Place:
@@ -140,7 +166,6 @@
         for q in PIECES:
             self.far[q].wait_recv()
             add_into(self.through(q), self.piece(q, self.next[q]))
-        for q in PIECES:
             self.passed[q].start()
 
     def finish(self):
@@ -164,8 +189,7 @@
     gate_ref,
     up_ref,
     down_ref,
-    out_ref,
-    grad_ref,
+    slots_ref,
     gate_w,
     up_w,
     down_w,
@@ -185,7 +209,6 @@
     send_sem,
     recv_sem,
     load_sem,
-    store_sem,
 ):
     place = Place(sections)
     links = Links(send_sem, recv_sem)
@@ -213,18 +236,7 @@
     load_acts.start()
     load_cots.start()
 
-    chosen = ids_ref[...] == 0
-    flags = jnp.where(chosen, 1.0, 0.0).astype(F32)
-    weights = jnp.where(chosen, probs_ref[...], 0.0)
-    picked = jnp.broadcast_to(flags[0:1] + flags[1:2], (8, toks))
-    share = jnp.broadcast_to(weights[0:1] + weights[1:2], (8, toks))
-    earlier = lax.broadcasted_iota(jnp.int32, (toks, toks), 0) < lax.broadcasted_iota(
-        jnp.int32, (toks, toks), 1
-    )
-    rank = dot_nn(picked.astype(BF16), jnp.where(earlier, 1.0, 0.0).astype(BF16))
-    slot = jnp.where(picked > 0.5, rank, -1.0)
-    line = lax.broadcasted_iota(jnp.int32, (8, toks), 0)
-    info[0] = jnp.where(line == 0, slot, share)
+    info[0] = routing(ids_ref[...], probs_ref[...])
 
     pl.semaphore_wait(barrier, len(around))
     info_back = links.copy(info.at[0], info.at[1], place.other_section(sections - 1))
@@ -232,21 +244,12 @@
     info_back.start()
     info_on.start()
 
-    def selection(block):
-        slot_line = block[0:1, :]
-        share_line = block[1:2, :]
-        number = lax.broadcasted_iota(jnp.int32, (CAP, toks), 0).astype(F32)
-        hit = number == slot_line
-        pick = jnp.where(hit, 1.0, 0.0).astype(BF16)
-        slot_share = jnp.sum(jnp.where(hit, share_line, 0.0), axis=1, keepdims=True)
-        return pick, slot_share
-
     def own_slot(rows, h, q):
         return rows.at[h, q, place.outer(h), place.inner(h)]
 
     load_acts.wait()
     info_back.wait_recv()
-    pick, _ = selection(info[1])
+    pick, _ = selection(toks, info[1])
     send_x = {}
     for h, q in CORNERS:
         part[h, q, 0, 0] = dot_nn(pick, down_w[pl.ds(0, toks), span(h, q)]).astype(BF16)
@@ -257,7 +260,7 @@
 
     load_cots.wait()
     info_on.wait_recv()
-    pick, slot_share = selection(info[2])
+    pick, slot_share = selection(toks, info[2])
     send_g = {}
     for h, q in CORNERS:
         chosen_rows = dot_nn(pick, down_w[pl.ds(toks, toks), span(h, q)])
@@ -353,20 +356,8 @@
 
     lax.fori_loop(0, SIDE, forward_terms, 0)
 
-    def reduces(rows, which):
-        first = [
-            ReduceRing(
-                place,
-                links,
-                h,
-                2,
-                lambda q, j, h=h: rows.at[h, q, j],
-                lambda q, h=h: thru_big.at[which, h, q],
-                lambda way, q, h=h: land_big.at[which, h, way, q],
-            )
-            for h in HALVES
-        ]
-        second = [
+    def second_sums(rows, which):
+        return [
             ReduceRing(
                 place,
                 links,
@@ -378,7 +369,40 @@
             )
             for h in HALVES
         ]
-        return first, second
+
+    first_o = [
+        ReduceRing(
+            place,
+            links,
+            h,
+            2,
+            lambda q, j, h=h: part.at[h, q, j],
+            lambda q, h=h: thru_big.at[0, h, q],
+            lambda way, q, h=h: land_big.at[0, h, way, q],
+        )
+        for h in HALVES
+    ]
+    second_o = second_sums(part, 0)
+
+    def block_of(h, n):
+        return (place.inner(h) + (2, 1, 3, 0)[n]) % SIDE
+
+    first_b = [
+        [
+            ReduceRing(
+                place,
+                links,
+                h,
+                2,
+                lambda q, j, h=h, n=n: rows_x.at[h, q, j, block_of(h, n)],
+                lambda q, h=h, n=n: thru_big.at[1, h, q, n],
+                lambda way, q, h=h, n=n: land_big.at[1, h, way, q, n],
+            )
+            for h in HALVES
+        ]
+        for n in range(SIDE)
+    ]
+    second_b = second_sums(rows_x, 1)
 
     def add_big(into, term):
         def step(j, carry):
@@ -390,21 +414,20 @@
     def add_small(into, term):
         into[...] = (into[...].astype(F32) + term[...].astype(F32)).astype(BF16)
 
-    def close_first(rows, which, h):
+    def close_block(rows, which, h, j, n):
         mine = place.outer(h)
-
+        for q in PIECES:
+            total = rows[h, q, mine, j].astype(F32)
+            for way in (0, 1):
+                total += land_big[which, h, way, q, n].astype(F32)
+            rows[h, q, mine, j] = total.astype(BF16)
+
+    def close_first(h):
         def step(j, carry):
-            for q in PIECES:
-                total = rows[h, q, mine, j].astype(F32)
-                for way in (0, 1):
-                    total += land_big[which, h, way, q, j].astype(F32)
-                rows[h, q, mine, j] = total.astype(BF16)
+            close_block(part, 0, h, j, j)
             return carry
 
         lax.fori_loop(0, SIDE, step, 0)
-
-    first_o, second_o = reduces(part, 0)
-    first_b, second_b = reduces(rows_x, 1)
 
     for h in HALVES:
         first_o[h].start()
@@ -444,62 +467,92 @@
 
     lax.fori_loop(0, SIDE, backward_terms, 0)
 
-    for h in HALVES:
-        first_b[h].start_far()
-
-    local_pick, local_share = selection(info[0])
-
-    def close_second(rows, which, h, q, staged):
+    for rings in first_b:
+        for h in HALVES:
+            rings[h].start_far()
+
+    _, local_share = selection(toks, info[0])
+
+    def close_second(rows, which, h, q):
         total = rows[h, q, place.outer(h), place.inner(h)].astype(F32)
         for way in (0, 1):
             total += land_small[which, h, way, q].astype(F32)
         if which == 0:
             total = total * local_share
-        spread = lax.dot_general(
-            local_pick, total.astype(BF16), (((0,), (0,)), ((), ())), preferred_element_type=F32
-        )
-        down_w[pl.ds(staged, toks), span(h, q)] = spread.astype(BF16)
+        slots_ref[which, :, span(h, q)] = total.astype(BF16)
 
     def close(rows, which, second):
         for h in HALVES:
             second[h].finish()
             for q in PIECES:
-                close_second(rows, which, h, q, which * toks)
+                close_second(rows, which, h, q)
+
+    def pass_block(n):
+        for h in HALVES:
+            first_b[n][h].start_near()
+        for h in HALVES:
+            first_b[n][h].relay(add_small)
+
+    def finish_block(n, h):
+        first_b[n][h].finish()
+        close_block(rows_x, 1, h, block_of(h, n), n)
 
     for h in HALVES:
         first_o[h].finish()
-        close_first(part, 0, h)
+        close_first(h)
         second_o[h].start()
-    for h in HALVES:
-        first_b[h].start_near()
-    for h in HALVES:
-        first_b[h].relay(add_big)
+    pass_block(0)
+    pass_block(1)
     for h in HALVES:
         second_o[h].relay(add_small)
+    pass_block(2)
+    for h in HALVES:
+        finish_block(0, h)
+        second_b[h].start_far()
+    for h in HALVES:
+        finish_block(1, h)
+        second_b[h].near[0].start()
+    pass_block(3)
+    for h in HALVES:
+        finish_block(2, h)
+        second_b[h].near[1].start()
+    for h in HALVES:
+        second_b[h].relay(add_small)
     close(part, 0, second_o)
-    store_out = pltpu.make_async_copy(acts_here, out_ref, store_sem.at[0])
-    store_out.start()
-    for h in HALVES:
-        first_b[h].finish()
-        close_first(rows_x, 1, h)
-        second_b[h].start()
-    for h in HALVES:
-        second_b[h].relay(add_small)
+    for h in HALVES:
+        finish_block(3, h)
     close(rows_x, 1, second_b)
-    store_grad = pltpu.make_async_copy(cots_here, grad_ref, store_sem.at[1])
-    store_grad.start()
 
     info_back.wait_send()
     info_on.wait_send()
-    for rings in (first_g, second_g, first_o, second_o, first_b, second_b):
+    for rings in (first_g, second_g, first_o, second_o, *first_b, second_b):
         for h in HALVES:
             rings[h].wait_sends()
-    store_out.wait()
-    store_grad.wait()
     assert links.used == COPIES
 
 
-COPIES = 2 + 8 + 2 * 4 * 6 + 2 * 4 * 6
+def spread_kernel(slots_ref, ids_ref, probs_ref, out_ref, grad_ref, staged, store_sem):
+    toks, width = out_ref.shape
+    cols = width // 4
+    pick, _ = selection(toks, routing(ids_ref[...], probs_ref[...]))
+    stores = []
+    for which, target in enumerate((out_ref, grad_ref)):
+        for k in range(4):
+            here = pl.ds(k * cols, cols)
+            spread = lax.dot_general(
+                pick, slots_ref[which, :, here], (((0,), (0,)), ((), ())), preferred_element_type=F32
+            )
+            staged[which, k] = spread.astype(BF16)
+            store = pltpu.make_async_copy(
+                staged.at[which, k], target.at[:, here], store_sem.at[which, k]
+            )
+            store.start()
+            stores.append(store)
+    for store in stores:
+        store.wait()
+
+
+COPIES = 2 + 8 + 2 * 4 * 6 + 2 * 2 * 6 + 2 * 5 * 6
 
 
 def body(sections, sent_acts, sent_cots, expert_ids, gate_probs, gate_weight, up_weight, down_weight):
@@ -512,14 +565,11 @@
     hbm = pl.BlockSpec(memory_space=pl.ANY)
     vmem = pl.BlockSpec(memory_space=pltpu.VMEM)
     block = (CAP, cols)
-    out_acts, in_grads = pl.pallas_call(
+    slots = pl.pallas_call(
         functools.partial(kernel, sections),
-        out_shape=(
-            jax.ShapeDtypeStruct((toks, width), BF16),
-            jax.ShapeDtypeStruct((toks, width), BF16),
-        ),
+        out_shape=pltpu.VMEM((2, CAP, width), BF16),
         in_specs=[hbm, hbm, vmem, vmem, hbm, hbm, hbm],
-        out_specs=(hbm, hbm),
+        out_specs=vmem,
         scratch_shapes=[
             pltpu.VMEM((width, units), BF16),
             pltpu.VMEM((width, units), BF16),
@@ -540,12 +590,25 @@
             pltpu.SemaphoreType.DMA((COPIES,)),
             pltpu.SemaphoreType.DMA((COPIES,)),
             pltpu.SemaphoreType.DMA((5,)),
-            pltpu.SemaphoreType.DMA((2,)),
         ],
         compiler_params=pltpu.CompilerParams(
-            collective_id=0, has_side_effects=True, vmem_limit_bytes=67043328
+            collective_id=0, has_side_effects=True, vmem_limit_bytes=63000000
         ),
     )(acts, cots, ids, probs, gate_weight[0], up_weight[0], down_weight[0])
+    out_acts, in_grads = pl.pallas_call(
+        spread_kernel,
+        out_shape=(
+            jax.ShapeDtypeStruct((toks, width), BF16),
+            jax.ShapeDtypeStruct((toks, width), BF16),
+        ),
+        in_specs=[vmem, vmem, vmem],
+        out_specs=(hbm, hbm),
+        scratch_shapes=[
+            pltpu.VMEM((2, 4, toks, cols), BF16),
+            pltpu.SemaphoreType.DMA((2, 4)),
+        ],
+        compiler_params=pltpu.CompilerParams(vmem_limit_bytes=8 << 20),
+    )(slots, ids, probs)
     return (out_acts[None], in_grads[None])
 
 

time: 184 us -> 178 us (0.967)
  local copies, waits for them, and re-layouts: 3.95 us -> 0.01 us
  Pallas kernels: 179 us -> 177 us
    unnamed x4, local copies, waits for them, and re-layouts: 3.95 us -> 0.01 us
    pallas_call x1 -> x2, Pallas kernels: 179 us -> 177 us  [the longest x1 175 us: body(): pl.pallas_call(functools.partial(kernel, sections), out_shape=pltpu.VMEM(...]
where the time goes in v3:
time: 178 us
  Pallas kernels  177 us (99%)
    pallas_call x1, Pallas kernels, body(): pl.pallas_call(functools.partial(kernel, sections), out_shape=pltpu.VMEM(...  175 us

profile of v3, /device:TPU:0, one launch (start us, length us, event | category | flops | bytes accessed | tf_op | source)
XLA Modules:
  0.0 177.5 jit_solution(10866877972295626928)
XLA Ops:
  0.6 0.0 copy-start
  0.6 0.0 copy-start.1
  0.7 174.7 %shard_map.86.slots_ref = bf16[2,40,6144]{2,1,0:T(8,128)(2,1)S(1)} custom-call(bf16[128,6144]{1,0:T(8,128)(2,1)} %bitcast.20, bf16[128,6144]{1,0:T(8,128)(2,1)} %bitcast.21, s32[2,128]{1,0:T(2,128)} %bitcast.13, f32[2,128]{1,0:T(2,128)} %bitcast.15, bf16[6144,512]{1,0:T(8,128)(2,1)} %bitcast.17, bf16[6144,512]{1,0:T(8,128)(2,1)} %bitcast.18, ...), custom_call_target="tpu_custom_call" | custom-call | tf_op jit(solution)/shard_map/pallas_call | solution.py:568
  175.3 0.0 copy-done
  175.3 0.0 copy-done.1
  175.4 2.2 %shard_map.87 = (bf16[128,6144]{1,0:T(8,128)(2,1)}, bf16[128,6144]{1,0:T(8,128)(2,1)}) custom-call(bf16[2,40,6144]{2,1,0:T(8,128)(2,1)S(1)} %shard_map.86.slots_ref, s32[2,128]{1,0:T(2,128)S(1)} %bitcast.14, f32[2,128]{1,0:T(2,128)S(1)} %bitcast.16), custom_call_target="tpu_custom_call" | custom-call | tf_op jit(solution)/shard_map/pallas_call | solution.py:598
Async XLA Ops:
  0.6 174.7 %copy-start = (s32[1,128,2]{1,2,0:T(2,128)S(1)}, s32[1,128,2]{1,2,0:T(2,128)}, u32[]{:S(2)}) copy-start(s32[1,128,2]{1,2,0:T(2,128)} %param.9) | copy-start | bytes 3076
  0.6 174.7 %copy-start.1 = (f32[1,128,2]{1,2,0:T(2,128)S(1)}, f32[1,128,2]{1,2,0:T(2,128)}, u32[]{:S(2)}) copy-start(f32[1,128,2]{1,2,0:T(2,128)} %param.10) | copy-start | bytes 3076
